TPU v7x, 256 devices: a whole 4x4x8 slice. The times are simulated.
256 devices in a mesh: layer: 2 (over x_lo), row: 32 (over z, y), col: 4 (over x_hi, core).
Axes of the slice: x: 4 (x_hi: 2, x_lo: 2; x = x_hi * 2 + x_lo), y: 4, z: 8, core: 2. Of those that a mesh axis runs over, the one named last changes fastest.
Arguments:
- rhs_root: float32 [16384, 128], P('col'), may hold values from -6 to 6
- rhs_child: float32 [2, 8192, 128], P('layer', 'col'), may hold values from -6 to 6
- rhs_leaf: float32 [4, 4096, 128], P('layer', 'col'), may hold values from -6 to 6
- root_inv: bfloat16 [16384, 16384], P('row', 'col'), may hold values from -0.046875 to 0.046875
- child_inv: bfloat16 [2, 8192, 8192], P('layer', 'row', 'col'), may hold values from -0.0625 to 0.0625
- leaf_inv: bfloat16 [4, 4096, 4096], P('layer', 'row', 'col'), may hold values from -0.09375 to 0.09375
- leaf_to_child: bfloat16 [4, 8192, 4096], P('layer', 'col', 'row'), may hold values from -0.0625 to 0.0625
- leaf_to_root: bfloat16 [4, 16384, 4096], P('layer', 'col', 'row'), may hold values from -0.03125 to 0.03125
- child_to_root: bfloat16 [2, 16384, 8192], P('layer', 'col', 'row'), may hold values from -0.03125 to 0.03125
Outputs:
- x_root: float32 [16384, 128], P('col')
- x_child: float32 [2, 8192, 128], P('layer', 'col')
- x_leaf: float32 [4, 4096, 128], P('layer', 'col')
- y_root: float32 [16384, 128], P('row')
All inputs are finite; a program needn't handle non-finite values.
Results may differ from a plain program's by a relative error of at most 0.008.
Values sent between devices are 32-bit elements; how exact they have to be, the bound alone decides.
No kernel may reach another device: no remote copies, remote signals or barrier semaphores. Data moves between devices by JAX's collectives and lax.ppermute only.
A program may use at most 64 MiB of HBM per device.

v0:
```python
import jax
import jax.numpy as jnp
from jax import lax
from jax.sharding import PartitionSpec as P


def col_sum(values):
    return lax.psum(values, "col")


def row_sum(values):
    return lax.psum(values, "row")


def root_total(values):
    return lax.psum(values, ("layer", "row"))


def half16(values):
    return values.astype(jnp.bfloat16)


def on_device(
    rhs_root,
    rhs_child,
    rhs_leaf,
    root_inv,
    child_inv,
    leaf_inv,
    leaf_to_child,
    leaf_to_root,
    child_to_root,
):
    f32 = jnp.float32
    y_leaf = col_sum(
        jnp.einsum("gij,gjs->gis", leaf_inv, half16(rhs_leaf), preferred_element_type=f32)
    )
    leaf_bf = half16(y_leaf)
    leaf_update = jnp.einsum("gij,gjs->is", leaf_to_root, leaf_bf, preferred_element_type=f32)
    r_child = rhs_child[0] - row_sum(
        jnp.einsum("gij,gjs->is", leaf_to_child, leaf_bf, preferred_element_type=f32)
    )
    y_child = col_sum(jnp.dot(child_inv[0], half16(r_child), preferred_element_type=f32))
    child_update = jnp.dot(child_to_root[0], half16(y_child), preferred_element_type=f32)
    r_root = rhs_root - root_total(child_update + leaf_update)
    y_root = col_sum(jnp.dot(root_inv, half16(r_root), preferred_element_type=f32))
    x_root = row_sum(jnp.einsum("ij,is->js", root_inv, half16(y_root), preferred_element_type=f32))
    root_bf = half16(x_root)
    back_child = y_child - col_sum(
        jnp.einsum("ij,is->js", child_to_root[0], root_bf, preferred_element_type=f32)
    )
    x_child = row_sum(
        jnp.einsum("ij,is->js", child_inv[0], half16(back_child), preferred_element_type=f32)
    )
    terms = jnp.einsum("gij,is->gjs", leaf_to_child, half16(x_child), preferred_element_type=f32)
    terms = terms + jnp.einsum("gij,is->gjs", leaf_to_root, root_bf, preferred_element_type=f32)
    back_leaf = y_leaf - col_sum(terms)
    x_leaf = row_sum(
        jnp.einsum("gij,gis->gjs", leaf_inv, half16(back_leaf), preferred_element_type=f32)
    )
    return (x_root, x_child[None], x_leaf, y_root)


def solution(mesh):
    in_specs = (
        P("col", None),
        P("layer", "col", None),
        P("layer", "col", None),
        P("row", "col"),
        P("layer", "row", "col"),
        P("layer", "row", "col"),
        P("layer", "col", "row"),
        P("layer", "col", "row"),
        P("layer", "col", "row"),
    )
    out_specs = (P("col", None), P("layer", "col", None), P("layer", "col", None), P("row", None))
    return jax.shard_map(
        on_device, mesh=mesh, in_specs=in_specs, out_specs=out_specs, check_vma=False
    )
```

profile of v0, /device:TPU:2, one launch (start us, length us, event | category | flops | bytes accessed | tf_op | source)
XLA Modules:
  0.0 1495.1 jit_solution(6463682180785090896)
XLA Ops:
  7.2 2.5 fusion.18
  9.7 0.0 all-reduce.13.cloned.1.call-start
  9.8 48.8 %all-reduce.11.cloned.1.call-done = f32[2,128,128]{2,1,0:T(8,128)} async-done(((f32[2,128,128]{2,1,0:T(8,128)}), f32[2,128,128]{2,1,0:T(8,128)}) %all-reduce.11.cloned.1.call-update) | async-done | bytes 131088 | tf_op jit(solution)/shard_map/psum | solution.py:8
  58.5 2.6 convolution_bitcast_fusion.2
  61.2 0.0 all-reduce.15.cloned.1.call-start
  61.2 152.3 %all-reduce.13.cloned.1.call-done = f32[2048,128]{1,0:T(8,128)} async-done(((f32[2048,128]{1,0:T(8,128)}), f32[2048,128]{1,0:T(8,128)}) %all-reduce.13.cloned.1.call-update) | async-done | bytes 1048592 | tf_op jit(solution)/shard_map/psum | solution.py:12
  213.5 2.7 convolution_bitcast_fusion.6
  216.3 0.0 all-reduce.17.cloned.1.call-start
  216.3 3.6 convolution_bitcast_fusion
  219.9 38.4 %all-reduce.15.cloned.1.call-done = f32[256,128]{0,1:T(8,128)} async-done(((f32[256,128]{0,1:T(8,128)}), f32[256,128]{0,1:T(8,128)}) %all-reduce.15.cloned.1.call-update) | async-done | bytes 131088 | tf_op jit(solution)/shard_map/psum | solution.py:8
  258.3 3.7 fusion
  262.1 612.7 %all-reduce.17.cloned.1.call-done = f32[4096,128]{1,0:T(8,128)} async-done(((f32[4096,128]{1,0:T(8,128)}), f32[4096,128]{1,0:T(8,128)}) %all-reduce.17.cloned.1.call-update) | async-done | bytes 2097168 | tf_op jit(solution)/shard_map/psum | solution.py:16
  874.8 5.7 convolution_bitcast_fusion.5
  880.6 0.0 all-reduce.21.cloned.1.call-start
  880.6 43.7 %all-reduce.19.cloned.1.call-done = f32[512,128]{0,1:T(8,128)} async-done(((f32[512,128]{0,1:T(8,128)}), f32[512,128]{0,1:T(8,128)}) %all-reduce.19.cloned.1.call-update) | async-done | bytes 262160 | tf_op jit(solution)/shard_map/psum | solution.py:8
  924.4 4.3 convolution_bitcast_fusion.1
  928.7 0.0 all-reduce.23.cloned.1.call-start
  928.8 154.9 %all-reduce.21.cloned.1.call-done = f32[4096,128]{0,1:T(8,128)} async-done(((f32[4096,128]{0,1:T(8,128)}), f32[4096,128]{0,1:T(8,128)}) %all-reduce.21.cloned.1.call-update) | async-done | bytes 2097168 | tf_op jit(solution)/shard_map/psum | solution.py:12
  1083.7 2.7 fusion.4
  1086.5 42.2 %all-reduce.23.cloned.1.call-done = f32[256,128]{0,1:T(8,128)} async-done(((f32[256,128]{0,1:T(8,128)}), f32[256,128]{0,1:T(8,128)}) %all-reduce.23.cloned.1.call-update) | async-done | bytes 131088 | tf_op jit(solution)/shard_map/psum | solution.py:8
  1128.7 2.2 convolution_bitcast_fusion.3
  1130.9 0.0 all-reduce.27.cloned.1.call-start
  1131.0 152.7 %all-reduce.25.cloned.1.call-done = f32[2048,128]{0,1:T(8,128)} async-done(((f32[2048,128]{0,1:T(8,128)}), f32[2048,128]{0,1:T(8,128)}) %all-reduce.25.cloned.1.call-update) | async-done | bytes 1048592 | tf_op jit(solution)/shard_map/psum | solution.py:12
  1283.7 2.2 fusion.13
  1285.9 3.1 fusion.7
  1289.2 41.6 %all-reduce.27.cloned.1.call-done = f32[2,128,128]{2,1,0:T(8,128)} async-done(((f32[2,128,128]{2,1,0:T(8,128)}), f32[2,128,128]{2,1,0:T(8,128)}) %all-reduce.27.cloned.1.call-update) | async-done | bytes 131088 | tf_op jit(solution)/shard_map/psum | solution.py:8
  1330.8 2.2 convolution_bitcast_fusion.4
  1333.1 0.8 copy.17
  1333.9 3.0 copy.14
  1336.9 1.3 copy.15
  1338.2 147.5 %all-reduce.29.cloned.1.call-done = f32[2,1024,128]{1,2,0:T(8,128)} async-done(((f32[2,1024,128]{1,2,0:T(8,128)}), f32[2,1024,128]{1,2,0:T(8,128)}) %all-reduce.29.cloned.1.call-update) | async-done | bytes 1048592 | tf_op jit(solution)/shard_map/psum | solution.py:12
  1485.7 2.5 copy.16
  (30 shorter events, 0.4 us)
Async XLA Ops:
  7.2 251.2 %copy-start = (bf16[1,4096,256]{2,1,0:T(8,128)(2,1)S(1)}, bf16[1,4096,256]{2,1,0:T(8,128)(2,1)}, u32[]{:S(2)}) copy-start(bf16[1,4096,256]{2,1,0:T(8,128)(2,1)} %param.17) | copy-start | bytes 6291460
  7.2 51.4 %all-reduce.11.cloned.1.call-start = ((), (), s32[]{:S(2)}) async-start(), calls=%async_computation | async-start | bytes 262144 | tf_op jit(solution)/shard_map/psum | solution.py:8
  9.7 203.8 %copy-start.2 = (bf16[1,256,2048]{2,1,0:T(8,128)(2,1)S(1)}, bf16[1,256,2048]{2,1,0:T(8,128)(2,1)}, u32[]{:S(2)}) copy-start(bf16[1,256,2048]{2,1,0:T(8,128)(2,1)} %param.13) | copy-start | bytes 3145732
  9.7 203.8 %all-reduce.13.cloned.1.call-start = ((), (), s32[]{:S(2)}) async-start(), calls=%async_computation.1 | async-start | bytes 2097152 | tf_op jit(solution)/shard_map/psum | solution.py:12
  61.2 155.1 %copy-start.5 = (f32[2,128,128]{2,1,0:T(8,128)S(1)}, f32[2,128,128]{2,1,0:T(8,128)}, u32[]{:S(2)}) copy-start(f32[2,128,128]{2,1,0:T(8,128)} %all-reduce.11.cloned.1.call-done) | copy-start | bytes 393220
  61.2 197.1 %all-reduce.15.cloned.1.call-start = ((), (), s32[]{:S(2)}) async-start(), calls=%async_computation.2 | async-start | bytes 262144 | tf_op jit(solution)/shard_map/psum | solution.py:8
  216.3 658.6 %all-reduce.17.cloned.1.call-start = ((), (), s32[]{:S(2)}) async-start(), calls=%async_computation.3 | async-start | bytes 4194304 | tf_op jit(solution)/shard_map/psum | solution.py:16
  262.0 662.3 %all-reduce.19.cloned.1.call-start = ((), (), s32[]{:S(2)}) async-start(), calls=%async_computation.4 | async-start | bytes 524288 | tf_op jit(solution)/shard_map/psum | solution.py:8
  880.6 203.1 %all-reduce.21.cloned.1.call-start = ((), (), s32[]{:S(2)}) async-start(), calls=%async_computation.5 | async-start | bytes 4194304 | tf_op jit(solution)/shard_map/psum | solution.py:12
  928.7 200.0 %copy-start.7 = (f32[256,128]{0,1:T(8,128)S(1)}, f32[256,128]{0,1:T(8,128)}, u32[]{:S(2)}) copy-start(f32[256,128]{0,1:T(8,128)} %all-reduce.15.cloned.1.call-done) | copy-start | bytes 393220
  928.7 200.0 %all-reduce.23.cloned.1.call-start = ((), (), s32[]{:S(2)}) async-start(), calls=%async_computation.6 | async-start | bytes 262144 | tf_op jit(solution)/shard_map/psum | solution.py:8
  1086.4 197.3 %all-reduce.25.cloned.1.call-start = ((), (), s32[]{:S(2)}) async-start(), calls=%async_computation.7 | async-start | bytes 2097152 | tf_op jit(solution)/shard_map/psum | solution.py:12
  1130.9 199.9 %all-reduce.27.cloned.1.call-start = ((), (), s32[]{:S(2)}) async-start(), calls=%async_computation.8 | async-start | bytes 262144 | tf_op jit(solution)/shard_map/psum | solution.py:8
  1283.7 2.2 copy-start.1
  1285.9 44.9 %copy-start.4 = (bf16[2,128,1024]{2,1,0:T(8,128)(2,1)S(1)}, bf16[2,128,1024]{2,1,0:T(8,128)(2,1)}, u32[]{:S(2)}) copy-start(bf16[2,128,1024]{2,1,0:T(8,128)(2,1)} %param.14) | copy-start | bytes 1572868
  1289.1 44.0 %copy-start.6 = (f32[512,128]{0,1:T(8,128)S(1)}, f32[512,128]{0,1:T(8,128)}, u32[]{:S(2)}) copy-start(f32[512,128]{0,1:T(8,128)} %all-reduce.19.cloned.1.call-done) | copy-start | bytes 786436
  1289.1 196.6 %all-reduce.29.cloned.1.call-start = ((), (), s32[]{:S(2)}) async-start(), calls=%async_computation.9 | async-start | bytes 2097152 | tf_op jit(solution)/shard_map/psum | solution.py:12
  1333.9 3.0 copy-start.3
Sparse Core Ops, SparseCore 0:
  11.2 47.3 all-reduce.10
  62.6 150.9 all-reduce.12
  216.7 41.5 all-reduce.14
  262.2 612.6 all-reduce.16
  880.7 43.6 all-reduce.18
  928.8 154.8 all-reduce.20
  1086.9 41.7 all-reduce.22
  1132.7 150.9 all-reduce.24
  1289.2 41.5 all-reduce.26
  1334.7 150.9 all-reduce.28
where the time goes:
time: 1500 us
  waiting for transfers between devices  1440 us (96%)
  matrix products  37.6 us (3%)
    psum x1, waiting for transfers between devices, root_total(): return lax.psum(values, ('layer', 'row'))  613 us
    psum x4, waiting for transfers between devices, row_sum(): return lax.psum(values, 'row')  607 us
    psum x5, waiting for transfers between devices, col_sum(): return lax.psum(values, 'col')  215 us
  transfers between devices with their start and end apart: 10, of which 10 were waited for; matrix products, arithmetic and copies ran while one was open for 1% of the time, Pallas kernels for 0%

commit v1 on v0

--- a/solution.py
+++ b/solution.py
@@ -5,7 +5,12 @@
 
 
 def col_sum(values):
-    return lax.psum(values, "col")
+
+    def wait_pages(t0):
+        block_out = jnp.sum(lax.all_gather(t0, "col"), axis=0)
+        return block_out
+
+    return wait_pages(values)
 
 
 def row_sum(values):

time: 1500 us -> 1330 us (0.89)
  waiting for transfers between devices: 1440 us -> 1230 us
  blocking collectives: 0 us -> 33.8 us
    psum x5 -> x0, waiting for transfers between devices: 215 us -> none  [col_sum(): return lax.psum(values, 'col')]
    all_gather x0 -> x4, blocking collectives: none -> 33.8 us  [wait_pages(): block_out = jnp.sum(lax.all_gather(t0, 'col'), axis=0)]
    all_gather x0 -> x1, waiting for transfers between devices: none -> 21.3 us  [wait_pages(): block_out = jnp.sum(lax.all_gather(t0, 'col'), axis=0)]
  transfers between devices with their start and end apart: 10 -> 6, of which waited for: 10 -> 6; matrix products, arithmetic and copies ran while one was open for 1% -> 1% of each run, Pallas kernels for 0% -> 0%
where the time goes in v1:
time: 1330 us
  waiting for transfers between devices  1230 us (92%)
  blocking collectives  33.8 us (3%)
  matrix products  33.2 us (2%)
  local copies, waits for them, and re-layouts  15.7 us (1%)
  between operations  14.2 us (1%)
    psum x1, waiting for transfers between devices, root_total(): return lax.psum(values, ('layer', 'row'))  609 us
    psum x4, waiting for transfers between devices, row_sum(): return lax.psum(values, 'row')  596 us
    all_gather x4, blocking collectives, wait_pages(): block_out = jnp.sum(lax.all_gather(t0, 'col'), axis=0)  33.8 us
  transfers between devices with their start and end apart: 6, of which 6 were waited for; matrix products, arithmetic and copies ran while one was open for 1% of the time, Pallas kernels for 0%

profile of v1, /device:TPU:2, one launch (start us, length us, event | category | flops | bytes accessed | tf_op | source)
XLA Modules:
  0.0 1330.6 jit_solution(14329407301621851748)
XLA Ops:
  7.2 1.9 fusion.18
  9.1 8.7 all-gather
  17.8 1.1 reduce_sum.45
  18.9 1.4 convolution_bitcast_fusion.2
  20.4 3.7 convolution_bitcast_fusion
  24.1 149.9 %all-reduce.6.cloned.1.call-done = f32[2048,128]{1,0:T(8,128)} async-done(((f32[2048,128]{1,0:T(8,128)}), f32[2048,128]{1,0:T(8,128)}) %all-reduce.6.cloned.1.call-update) | async-done | bytes 1048592 | tf_op jit(solution)/shard_map/psum | solution.py:17
  174.0 2.0 convolution_bitcast_fusion.6
  176.0 8.5 all-gather.1
  184.5 2.1 reshape.9
  186.6 1.4 reduce_sum.46
  187.9 3.7 fusion
  191.7 609.5 %all-reduce.8.cloned.1.call-done = f32[4096,128]{1,0:T(8,128)} async-done(((f32[4096,128]{1,0:T(8,128)}), f32[4096,128]{1,0:T(8,128)}) %all-reduce.8.cloned.1.call-update) | async-done | bytes 2097168 | tf_op jit(solution)/shard_map/psum | solution.py:21
  801.2 5.7 convolution_bitcast_fusion.5
  806.9 21.3 %all-gather.7.cloned.1.call-done = f32[2048,128]{0,1:T(8,128)} async-done(((f32[512,128]{0,1:T(8,128)}), f32[2048,128]{0,1:T(8,128)}) %all-gather.7.cloned.1.call-update) | async-done | bytes 1048592 | tf_op jit(solution)/shard_map/all_gather | solution.py:10
  828.2 2.9 reshape.10
  831.1 1.8 reduce_sum.47
  833.0 4.2 convolution_bitcast_fusion.1
  837.3 154.9 %all-reduce.10.cloned.1.call-done = f32[4096,128]{0,1:T(8,128)} async-done(((f32[4096,128]{0,1:T(8,128)}), f32[4096,128]{0,1:T(8,128)}) %all-reduce.10.cloned.1.call-update) | async-done | bytes 2097168 | tf_op jit(solution)/shard_map/psum | solution.py:17
  992.2 2.0 fusion.4
  994.3 8.5 all-gather.3
  1002.7 2.1 reshape.11
  1004.8 2.0 reduce_sum.48
  1006.8 2.2 convolution_bitcast_fusion.3
  1009.1 148.0 %all-reduce.12.cloned.1.call-done = f32[2048,128]{0,1:T(8,128)} async-done(((f32[2048,128]{0,1:T(8,128)}), f32[2048,128]{0,1:T(8,128)}) %all-reduce.12.cloned.1.call-update) | async-done | bytes 1048592 | tf_op jit(solution)/shard_map/psum | solution.py:17
  1157.1 2.0 fusion.13
  1159.3 2.1 fusion.7
  1162.2 8.2 all-gather.4
  1171.1 2.2 convolution_bitcast_fusion.4
  1174.2 3.0 copy.18
  1177.1 1.3 copy.19
  1178.4 142.7 %all-reduce.14.cloned.1.call-done = f32[2,1024,128]{1,2,0:T(8,128)} async-done(((f32[2,1024,128]{1,2,0:T(8,128)}), f32[2,1024,128]{1,2,0:T(8,128)}) %all-reduce.14.cloned.1.call-update) | async-done | bytes 1048592 | tf_op jit(solution)/shard_map/psum | solution.py:17
  1321.2 2.5 copy.20
  (29 shorter events, 2.9 us)
Async XLA Ops:
  7.2 180.8 %copy-start = (bf16[1,4096,256]{2,1,0:T(8,128)(2,1)S(1)}, bf16[1,4096,256]{2,1,0:T(8,128)(2,1)}, u32[]{:S(2)}) copy-start(bf16[1,4096,256]{2,1,0:T(8,128)(2,1)} %param.17) | copy-start | bytes 6291460
  7.2 11.7 copy-start.3
  7.2 166.8 %all-reduce.6.cloned.1.call-start = ((), (), s32[]{:S(2)}) async-start(), calls=%async_computation | async-start | bytes 2097152 | tf_op jit(solution)/shard_map/psum | solution.py:17
  20.3 153.7 %copy-start.2 = (bf16[1,256,2048]{2,1,0:T(8,128)(2,1)S(1)}, bf16[1,256,2048]{2,1,0:T(8,128)(2,1)}, u32[]{:S(2)}) copy-start(bf16[1,256,2048]{2,1,0:T(8,128)(2,1)} %param.13) | copy-start | bytes 3145732
  20.4 780.8 %all-reduce.8.cloned.1.call-start = ((), (), s32[]{:S(2)}) async-start(), calls=%async_computation.1 | async-start | bytes 4194304 | tf_op jit(solution)/shard_map/psum | solution.py:21
  187.9 3.7 copy-start.6
  191.6 636.6 %all-gather.7.cloned.1.call-start = ((), (), s32[]{:S(2)}) async-start(), calls=%async_computation.5 | async-start | bytes 1310720 | tf_op jit(solution)/shard_map/all_gather | solution.py:10
  806.9 185.3 %all-reduce.10.cloned.1.call-start = ((), (), s32[]{:S(2)}) async-start(), calls=%async_computation.2 | async-start | bytes 4194304 | tf_op jit(solution)/shard_map/psum | solution.py:17
  837.2 319.9 %all-reduce.12.cloned.1.call-start = ((), (), s32[]{:S(2)}) async-start(), calls=%async_computation.3 | async-start | bytes 2097152 | tf_op jit(solution)/shard_map/psum | solution.py:17
  1009.1 312.1 %all-reduce.14.cloned.1.call-start = ((), (), s32[]{:S(2)}) async-start(), calls=%async_computation.4 | async-start | bytes 2097152 | tf_op jit(solution)/shard_map/psum | solution.py:17
  1157.1 2.2 copy-start.1
  1159.3 11.7 copy-start.5
  1174.2 3.0 copy-start.4
Sparse Core Ops, SparseCore 0:
  20.5 153.4 all-reduce.5
  191.8 609.3 all-reduce.7
  807.0 21.1 all-gather.6
  837.3 154.8 all-reduce.9
  1009.2 147.8 all-reduce.11
  1173.5 147.6 all-reduce.13
